TPU v7x, 32 devices: a whole 2x2x4 slice. The times are simulated.
32 devices in a mesh: wide: 8 (over z, y), narrow: 4 (over x, core).
Axes of the slice: x: 2, y: 2, z: 4, core: 2. Of those that a mesh axis runs over, the one named last changes fastest.
Arguments:
- stem: float32 [2, 8, 4, 512, 128], P(None, 'wide', 'narrow'), may hold values from -6 to 6
- branches: float32 [3, 2, 512, 512], replicated, may hold values from -0.1875 to 0.1875
- mode_order: int32 [3, 9], replicated, may hold values from 0 to 8, each once within a row
Outputs:
- final_stem: float32 [2, 8, 4, 512, 128], P(None, 'wide', 'narrow')
Inputs may be any that keep to these rules, and one draw needn't show every extreme that they name: Each row of mode_order names every mode of 0 to 8 once.
All inputs are finite; a program needn't handle non-finite values.
Results may differ from a plain program's by a relative error of at most 0.0003.
Values may be sent and summed in bfloat16 or wider, within the bound.
No kernel may reach another device: no remote copies, remote signals or barrier semaphores. Data moves between devices by JAX's collectives and lax.ppermute only.
A program may use at most 64 MiB of HBM per device.

v0:
```python
import jax
import jax.numpy as jnp
from jax import lax
from jax.sharding import PartitionSpec as P


def split_pair(values):
    high = values.astype(jnp.bfloat16)
    held = lax.optimization_barrier(high)
    low = (values - held.astype(jnp.float32)).astype(jnp.bfloat16)
    return (high, low)


def expand_order(order, columns):
    column = jnp.arange(columns, dtype=jnp.int32)
    places = jnp.arange(order.shape[0], dtype=jnp.int32)
    bits = jnp.bitwise_and(jnp.right_shift(column[:, None], places[None, :]), 1)
    return jnp.sum(jnp.left_shift(bits, order[None, :]), axis=1)


def prepare(branch_step, order):
    columns = branch_step.shape[1]
    bhigh, blow = split_pair(branch_step)
    inverse_order = jnp.argsort(order)
    inverse = expand_order(inverse_order, columns)
    return (bhigh.reshape(2 * columns, columns), blow.reshape(2 * columns, columns), inverse)


def mult(left, right):
    return lax.dot_general(
        left, right, (((0,), (0,)), ((), ())), preferred_element_type=jnp.float32
    )


def contract(stem_pieces, branch_pieces):
    shigh, slow = stem_pieces
    flat_high, flat_low, inverse = branch_pieces
    shigh = jnp.take(shigh, inverse, axis=1)
    slow = jnp.take(slow, inverse, axis=1)
    rows_count = shigh.shape[2]
    real_high = jnp.concatenate([shigh[0], -shigh[1]], axis=0)
    real_low = jnp.concatenate([slow[0], -slow[1]], axis=0)
    imag_high = jnp.concatenate([shigh[1], shigh[0]], axis=0)
    imag_low = jnp.concatenate([slow[1], slow[0]], axis=0)
    upper = mult(flat_high, jnp.concatenate([real_high, real_low, imag_high, imag_low], axis=1))
    lower = mult(flat_low, jnp.concatenate([real_high, imag_high], axis=1))
    real = upper[:, :rows_count] + upper[:, rows_count : 2 * rows_count] + lower[:, :rows_count]
    imag = (
        upper[:, 2 * rows_count : 3 * rows_count]
        + upper[:, 3 * rows_count :]
        + lower[:, rows_count:]
    )
    return jnp.stack([real, imag])


def body(stem, branches, mode_order):
    columns = stem.shape[3]
    rows_here = stem.shape[4]
    narrow_n = lax.axis_size("narrow")
    wide_n = lax.axis_size("wide")
    local = stem.reshape(2, columns, rows_here)
    first_branch = prepare(branches[0], mode_order[0])
    second_branch = prepare(branches[1], mode_order[1])
    third_branch = prepare(branches[2], mode_order[2])
    first = contract(split_pair(local), first_branch)
    outgoing = first.reshape(2, narrow_n, columns // narrow_n, rows_here)
    received = lax.all_to_all(outgoing, "narrow", split_axis=1, concat_axis=1, tiled=True)
    merged = received.reshape(2, columns, received.shape[3])
    second = contract(split_pair(merged), second_branch)
    outgoing = second.reshape(2, wide_n, columns // wide_n, rows_here)
    received = lax.all_to_all(outgoing, "wide", split_axis=1, concat_axis=1, tiled=True)
    merged = received.reshape(2, columns, received.shape[3])
    final = contract(split_pair(merged), third_branch)
    return final.reshape(2, 1, 1, columns, rows_here)


def solution(mesh):
    return jax.shard_map(
        body,
        mesh=mesh,
        in_specs=(P(None, "wide", "narrow", None, None), P(), P()),
        out_specs=P(None, "wide", "narrow", None, None),
        check_vma=False,
    )
```

profile of v0, /device:TPU:0, one launch (start us, length us, event | category | flops | bytes accessed | tf_op | source)
XLA Modules:
  0.0 81.4 jit_solution(7135167233199474065)
XLA Ops:
  0.0 0.8 slice_bitcast_fusion
  0.8 1.3 %sort.45 = (s32[9]{0:T(128)}, s32[9]{0:T(128)S(1)}) sort(s32[9]{0:T(128)S(1)} %get-tuple-element.52, s32[9]{0:T(128)S(1)} %iota.22), dimensions={0}, to_apply=%region_0.0 | sort | flops 36 | bytes 144 | tf_op jit(solution)/shard_map/jit(argsort)/sort | solution.py:24
  2.2 4.9 %fusion.95 = (bf16[1,2,512,512]{3,2,1,0:T(8,128)(2,1)}, bf16[2,512,512]{2,1,0:T(8,128)(2,1)S(1)}, bf16[2,512,512]{2,1,0:T(8,128)(2,1)S(1)}, bf16[2,512,512]{2,1,...) fusion(f32[3,2,512,512]{3,2,1,0:T(8,128)} %param.6), kind=kLoop, calls=%fused_computation.168 | loop fusion | bytes 9437184 | tf_op jit(solution)/shard_map/slice | solution.py:64
  7.4 1.2 %fusion.74 = bf16[2,512,128]{2,0,1:T(2,128)(2,1)} fusion(bf16[2,512,128]{2,0,1:T(2,128)(2,1)S(1)} %bitcast.121, f32[2,1,1,512,128]{4,3,2,1,0:T(8,128)S(1)} %copy-done), kind=kLoop, calls=%fused_computation.101 | loop fusion | flops 393216 | bytes 1048576 | tf_op jit(solution)/shard_map/convert_element_type | solution.py:10
  8.6 2.4 %gather_fusion = bf16[512,2,128]{2,1,0:T(2,128)(2,1)} fusion(bf16[2,512,128]{2,0,1:T(2,128)(2,1)S(1)} %bitcast.122, s32[1024]{0:T(1024)S(1)} %pad_clamp_fusion.2), kind=kCustom, calls=%fused_computation.clone | custom fusion | bytes 526336 | tf_op jit(solution)/shard_map/jit(_take)/gather | solution.py:38
  11.0 2.3 %gather_fusion.1 = bf16[512,2,128]{2,1,0:T(2,128)(2,1)S(1)} fusion(bf16[2,512,128]{2,0,1:T(2,128)(2,1)} %fusion.74, s32[1024]{0:T(1024)S(1)} %pad_clamp_fusion.2), kind=kCustom, calls=%fused_computation.1.clone | custom fusion | bytes 526336 | tf_op jit(solution)/shard_map/jit(_take)/gather | solution.py:39
  13.3 3.0 %fusion.78 = (bf16[2,512,128]{2,0,1:T(2,128)(2,1)S(1)}, bf16[2,512,128]{2,0,1:T(2,128)(2,1)S(1)}) fusion(bf16[512,2,128]{2,1,0:T(2,128)(2,1)S(1)} %gather_fusion.1, pred[512]{0:T(512)(128)(4,1)S(1)} %compare_and_fusion.2, bf16[512,2,128]{2,1,0:T(2,128)(2,1)} %gather_fusion), kind=kLoop, calls=%fused_computation.123 | loop fusion | flops 262144 | bytes 1049088 | tf_op jit(solution)/shard_map/jit(_take)/select_n | solution.py:39
  17.2 5.3 %fusion.2 = (bf16[2,512,512]{2,1,0:T(8,128)(2,1)S(1)}, bf16[2,512,512]{2,1,0:T(8,128)(2,1)}, bf16[2,512,512]{2,1,0:T(8,128)(2,1)}) fusion(bf16[2,512,512]{2,1,0:T(8,128)(2,1)S(1)} %get-tuple-element.25, f32[3,2,512,512]{3,2,1,0:T(8,128)} %param.6, bf16[2,512,512]{2,1,0:T(8,128)(2,1)S(1)} %get-tuple-element.26, bf16[2,512,512]{2,1,0:T(8,128)(2,1)S(1)} %get-tuple-element.27), kind=kLoop, calls=%fused_computation.14 | loop fusion | flops 4718592 | bytes 12582912 | tf_op jit(solution)/shard_map/convert_element_type | solution.py:10
  23.7 0.8 convolution_bitcast_fusion.2
  24.6 0.8 %pad_maximum_fusion = f32[2,4,128,128]{3,2,0,1:T(8,128)} fusion(f32[1,4,128,128]{3,2,0,1:T(8,128)S(1)} %bitcast.130, f32[1,4,128,128]{3,2,0,1:T(8,128)S(1)} %bitcast.129), kind=kLoop, calls=%fused_computation.74 | loop fusion | flops 131072 | bytes 1048576 | tf_op jit(solution)/shard_map/stack | solution.py:53
  25.4 4.2 %all-to-all-start = ((f32[2,4,128,128]{3,2,0,1:T(8,128)}), f32[2,4,128,128]{3,2,0,1:T(8,128)S(1)}, u32[]{:S(2)}, u32[]{:S(2)}) async-start(f32[2,4,128,128]{3,2,0,1:T(8,128)} %pad_maximum_fusion), calls=%async_computation | async-start | bytes 1048576 | tf_op jit(solution)/shard_map/all_to_all | solution.py:67
  29.6 1.2 %sort.46 = (s32[9]{0:T(128)}, s32[9]{0:T(128)S(1)}) sort(s32[9]{0:T(128)S(1)} %get-tuple-element.53, s32[9]{0:T(128)S(1)} %iota.23), dimensions={0}, to_apply=%region_2.0 | sort | flops 36 | bytes 144 | tf_op jit(solution)/shard_map/jit(argsort)/sort | solution.py:24
  31.0 7.5 %all-to-all-done = f32[2,4,128,128]{3,2,0,1:T(8,128)S(1)} async-done(((f32[2,4,128,128]{3,2,0,1:T(8,128)}), f32[2,4,128,128]{3,2,0,1:T(8,128)S(1)}, u32[]{:S(2)}, u32[]{:S(2)}) %all-to-all-start) | async-done | bytes 524320 | tf_op jit(solution)/shard_map/all_to_all | solution.py:67
  39.4 2.1 %gather_fusion.2 = bf16[512,2,128]{2,1,0:T(2,128)(2,1)S(1)} fusion(bf16[2,512,128]{2,0,1:T(2,128)(2,1)S(1)} %bitcast_convert_fusion.4, s32[1024]{0:T(1024)S(1)} %pad_clamp_fusion.1), kind=kCustom, calls=%fused_computation.2.clone | custom fusion | bytes 526336 | tf_op jit(solution)/shard_map/jit(_take)/gather | solution.py:38
  41.6 2.1 %gather_fusion.3 = bf16[512,2,128]{2,1,0:T(2,128)(2,1)S(1)} fusion(bf16[2,512,128]{2,0,1:T(2,128)(2,1)S(1)} %fusion.73, s32[1024]{0:T(1024)S(1)} %pad_clamp_fusion.1), kind=kCustom, calls=%fused_computation.3.clone | custom fusion | bytes 526336 | tf_op jit(solution)/shard_map/jit(_take)/gather | solution.py:39
  43.7 1.8 %fusion.80 = (bf16[2,512,128]{2,0,1:T(2,128)(2,1)S(1)}, bf16[2,512,128]{2,0,1:T(2,128)(2,1)S(1)}) fusion(bf16[512,2,128]{2,1,0:T(2,128)(2,1)S(1)} %gather_fusion.3, pred[512]{0:T(512)(128)(4,1)S(1)} %compare_and_fusion.1, bf16[512,2,128]{2,1,0:T(2,128)(2,1)S(1)} %gather_fusion.2), kind=kLoop, calls=%fused_computation.125 | loop fusion | flops 262144 | bytes 1049088 | tf_op jit(solution)/shard_map/jit(_take)/select_n | solution.py:39
  48.5 0.8 %pad_maximum_fusion.1 = f32[2,8,64,128]{3,2,0,1:T(8,128)} fusion(f32[1,8,64,128]{3,2,0,1:T(8,128)S(1)} %bitcast.132, f32[1,8,64,128]{3,2,0,1:T(8,128)S(1)} %bitcast.131), kind=kLoop, calls=%fused_computation.83 | loop fusion | flops 131072 | bytes 1048576 | tf_op jit(solution)/shard_map/stack | solution.py:53
  49.3 6.5 %all-to-all-start.1 = ((f32[2,8,64,128]{3,2,0,1:T(8,128)}), f32[2,8,64,128]{3,2,0,1:T(8,128)S(1)}, u32[]{:S(2)}, u32[]{:S(2)}) async-start(f32[2,8,64,128]{3,2,0,1:T(8,128)} %pad_maximum_fusion.1), calls=%async_computation.1 | async-start | bytes 1048576 | tf_op jit(solution)/shard_map/all_to_all | solution.py:71
  55.8 1.3 %sort.47 = (s32[9]{0:T(128)}, s32[9]{0:T(128)S(1)}) sort(s32[9]{0:T(128)S(1)} %get-tuple-element.51, s32[9]{0:T(128)S(1)} %iota.24), dimensions={0}, to_apply=%region_4.6 | sort | flops 36 | bytes 144 | tf_op jit(solution)/shard_map/jit(argsort)/sort | solution.py:24
  57.2 12.8 %all-to-all-done.1 = f32[2,8,64,128]{3,2,0,1:T(8,128)S(1)} async-done(((f32[2,8,64,128]{3,2,0,1:T(8,128)}), f32[2,8,64,128]{3,2,0,1:T(8,128)S(1)}, u32[]{:S(2)}, u32[]{:S(2)}) %all-to-all-start.1) | async-done | bytes 524320 | tf_op jit(solution)/shard_map/all_to_all | solution.py:71
  71.0 2.1 %gather_fusion.4 = bf16[512,2,128]{2,1,0:T(2,128)(2,1)S(1)} fusion(bf16[2,512,128]{2,0,1:T(2,128)(2,1)S(1)} %bitcast_convert_fusion.3, s32[1024]{0:T(1024)S(1)} %pad_clamp_fusion), kind=kCustom, calls=%fused_computation.4.clone | custom fusion | bytes 526336 | tf_op jit(solution)/shard_map/jit(_take)/gather | solution.py:38
  73.1 2.1 %gather_fusion.5 = bf16[512,2,128]{2,1,0:T(2,128)(2,1)S(1)} fusion(bf16[2,512,128]{2,0,1:T(2,128)(2,1)S(1)} %fusion.72, s32[1024]{0:T(1024)S(1)} %pad_clamp_fusion), kind=kCustom, calls=%fused_computation.5.clone | custom fusion | bytes 526336 | tf_op jit(solution)/shard_map/jit(_take)/gather | solution.py:39
  75.2 1.8 %fusion.82 = (bf16[2,512,128]{2,0,1:T(2,128)(2,1)S(1)}, bf16[2,512,128]{2,0,1:T(2,128)(2,1)S(1)}) fusion(bf16[512,2,128]{2,1,0:T(2,128)(2,1)S(1)} %gather_fusion.5, pred[512]{0:T(512)(128)(4,1)S(1)} %compare_and_fusion, bf16[512,2,128]{2,1,0:T(2,128)(2,1)S(1)} %gather_fusion.4), kind=kLoop, calls=%fused_computation.127 | loop fusion | flops 262144 | bytes 1049088 | tf_op jit(solution)/shard_map/jit(_take)/select_n | solution.py:39
  80.4 1.0 %copy.68 = f32[2,1,1,512,128]{4,3,2,1,0:T(8,128)} copy(f32[2,1,1,512,128]{3,4,0,2,1:T(8,128)S(1)} %maximum_bitcast_fusion) | data formatting | bytes 1048576 | tf_op jit(solution)/shard_map/reshape | solution.py:74
  (60 shorter events, 11.0 us)
Async XLA Ops:
  2.2 4.9 %copy-start = (f32[2,1,1,512,128]{4,3,2,1,0:T(8,128)S(1)}, f32[2,1,1,512,128]{4,3,2,1,0:T(8,128)}, u32[]{:S(2)}) copy-start(f32[2,1,1,512,128]{4,3,2,1,0:T(8,128)} %param.5) | copy-start | bytes 1572868
  22.5 1.2 %copy-start.5 = (bf16[1,2,512,512]{3,2,1,0:T(8,128)(2,1)S(1)}, bf16[1,2,512,512]{3,2,1,0:T(8,128)(2,1)}, u32[]{:S(2)}) copy-start(bf16[1,2,512,512]{3,2,1,0:T(8,128)(2,1)} %get-tuple-element.28) | copy-start | bytes 3145732
  25.4 13.1 %all-to-all-start = ((f32[2,4,128,128]{3,2,0,1:T(8,128)}), f32[2,4,128,128]{3,2,0,1:T(8,128)S(1)}, u32[]{:S(2)}, u32[]{:S(2)}) async-start(f32[2,4,128,128]{3,2,0,1:T(8,128)} %pad_maximum_fusion), calls=%async_computation | async-start | bytes 1048576 | tf_op jit(solution)/shard_map/all_to_all | solution.py:67
  45.5 1.2 %copy-start.4 = (bf16[2,512,512]{2,1,0:T(8,128)(2,1)S(1)}, bf16[2,512,512]{2,1,0:T(8,128)(2,1)}, u32[]{:S(2)}) copy-start(bf16[2,512,512]{2,1,0:T(8,128)(2,1)} %get-tuple-element.31) | copy-start | bytes 3145732
  46.3 1.3 %copy-start.3 = (bf16[1,2,512,512]{3,2,1,0:T(8,128)(2,1)S(1)}, bf16[1,2,512,512]{3,2,1,0:T(8,128)(2,1)}, u32[]{:S(2)}) copy-start(bf16[1,2,512,512]{3,2,1,0:T(8,128)(2,1)} %get-tuple-element.29) | copy-start | bytes 3145732
  49.3 20.7 %all-to-all-start.1 = ((f32[2,8,64,128]{3,2,0,1:T(8,128)}), f32[2,8,64,128]{3,2,0,1:T(8,128)S(1)}, u32[]{:S(2)}, u32[]{:S(2)}) async-start(f32[2,8,64,128]{3,2,0,1:T(8,128)} %pad_maximum_fusion.1), calls=%async_computation.1 | async-start | bytes 1048576 | tf_op jit(solution)/shard_map/all_to_all | solution.py:71
  77.0 1.2 %copy-start.2 = (bf16[2,512,512]{2,1,0:T(8,128)(2,1)S(1)}, bf16[2,512,512]{2,1,0:T(8,128)(2,1)}, u32[]{:S(2)}) copy-start(bf16[2,512,512]{2,1,0:T(8,128)(2,1)} %get-tuple-element.32) | copy-start | bytes 3145732
  78.2 1.2 %copy-start.1 = (bf16[1,2,512,512]{3,2,1,0:T(8,128)(2,1)S(1)}, bf16[1,2,512,512]{3,2,1,0:T(8,128)(2,1)}, u32[]{:S(2)}) copy-start(bf16[1,2,512,512]{3,2,1,0:T(8,128)(2,1)} %get-tuple-element.24) | copy-start | bytes 3145732
where the time goes:
time: 81.9 us; the launch traced here: 81.4 us
  local copies, waits for them, and re-layouts  25.9 us (32%)
  other arithmetic  20.5 us (25%)
  waiting for transfers between devices  20.3 us (25%)
  starting transfers between devices  10.7 us (13%)
  matrix products  3.67 us (4%)
    all_to_all x1, waiting for transfers between devices, body(): lax.all_to_all(outgoing, 'wide', split_axis=1, concat_axis=1, tiled=True)  12.8 us
    all_to_all x1, waiting for transfers between devices, body(): lax.all_to_all(outgoing, 'narrow', split_axis=1, concat_axis=1, tiled=True)  7.53 us
    convert_element_type x4, other arithmetic, split_pair(): low = (values - held.astype(jnp.float32)).astype(jnp.bfloat16)  7.11 us
    gather x3, local copies, waits for them, and re-layouts, contract(): shigh = jnp.take(shigh, inverse, axis=1)  6.6 us
    select_n x3, other arithmetic, contract(): slow = jnp.take(slow, inverse, axis=1)  6.55 us
    gather x3, local copies, waits for them, and re-layouts, contract(): slow = jnp.take(slow, inverse, axis=1)  6.53 us
    all_to_all x1, starting transfers between devices, body(): lax.all_to_all(outgoing, 'wide', split_axis=1, concat_axis=1, tiled=True)  6.47 us
    slice x1, local copies, waits for them, and re-layouts, body(): third_branch = prepare(branches[2], mode_order[2])  4.86 us
  transfers between devices with their start and end apart: 2, of which 2 were waited for; matrix products, arithmetic and copies ran while one was open for 3% of the time, Pallas kernels for 0%

commit v1 on v0

--- a/solution.py
+++ b/solution.py
@@ -2,6 +2,12 @@
 import jax.numpy as jnp
 from jax import lax
 from jax.sharding import PartitionSpec as P
+
+
+def trade_parts(x, name, split, join):
+    cells = jnp.split(x, lax.axis_size(name), axis=split)
+    received = lax.all_to_all(jnp.stack(cells), name, 0, 0)
+    return jnp.concatenate(received, axis=join)
 
 
 def split_pair(values):
@@ -68,7 +74,7 @@
     merged = received.reshape(2, columns, received.shape[3])
     second = contract(split_pair(merged), second_branch)
     outgoing = second.reshape(2, wide_n, columns // wide_n, rows_here)
-    received = lax.all_to_all(outgoing, "wide", split_axis=1, concat_axis=1, tiled=True)
+    received = trade_parts(outgoing, "wide", 1, 1)
     merged = received.reshape(2, columns, received.shape[3])
     final = contract(split_pair(merged), third_branch)
     return final.reshape(2, 1, 1, columns, rows_here)

time: 81.9 us -> 87.3 us (1.066)
  other arithmetic: 20.5 us -> 24.2 us
  waiting for transfers between devices: 20.3 us -> 21.7 us
    unnamed x0 -> x7, other arithmetic: none -> 4.44 us
    all_to_all x1, waiting for transfers between devices: 12.8 us -> 14.2 us  [trade_parts(): received = lax.all_to_all(jnp.stack(cells), name, 0, 0)]
    another operation x3 -> x2, other arithmetic: 1.82 us -> 0.98 us  [contract(): return jnp.stack([real, imag])]
  transfers between devices with their start and end apart: 2 -> 2, of which waited for: 2 -> 2; matrix products, arithmetic and copies ran while one was open for 3% -> 2% of each run, Pallas kernels for 0% -> 0%
where the time goes in v1:
time: 87.3 us; the launch traced here: 86.7 us
  local copies, waits for them, and re-layouts  26.1 us (30%)
  other arithmetic  24.2 us (28%)
  waiting for transfers between devices  21.7 us (25%)
  starting transfers between devices  10.7 us (12%)
  matrix products  3.66 us (4%)
    all_to_all x1, waiting for transfers between devices, trade_parts(): received = lax.all_to_all(jnp.stack(cells), name, 0, 0)  14.2 us
    all_to_all x1, waiting for transfers between devices, body(): lax.all_to_all(outgoing, 'narrow', split_axis=1, concat_axis=1, tiled=True)  7.49 us
    convert_element_type x4, other arithmetic, split_pair(): low = (values - held.astype(jnp.float32)).astype(jnp.bfloat16)  6.87 us
    gather x3, local copies, waits for them, and re-layouts, contract(): shigh = jnp.take(shigh, inverse, axis=1)  6.6 us
    select_n x3, other arithmetic, contract(): slow = jnp.take(slow, inverse, axis=1)  6.54 us
    gather x3, local copies, waits for them, and re-layouts, contract(): slow = jnp.take(slow, inverse, axis=1)  6.53 us
    all_to_all x1, starting transfers between devices, trade_parts(): received = lax.all_to_all(jnp.stack(cells), name, 0, 0)  6.47 us
    slice x1, local copies, waits for them, and re-layouts, body(): third_branch = prepare(branches[2], mode_order[2])  4.86 us
  transfers between devices with their start and end apart: 2, of which 2 were waited for; matrix products, arithmetic and copies ran while one was open for 2% of the time, Pallas kernels for 0%

profile of v1, /device:TPU:0, one launch (start us, length us, event | category | flops | bytes accessed | tf_op | source)
XLA Modules:
  0.0 86.7 jit_solution(8210169564710069178)
XLA Ops:
  0.0 0.8 slice_bitcast_fusion
  0.8 1.3 %sort.45 = (s32[9]{0:T(128)}, s32[9]{0:T(128)S(1)}) sort(s32[9]{0:T(128)S(1)} %get-tuple-element.52, s32[9]{0:T(128)S(1)} %iota.22), dimensions={0}, to_apply=%region_0.0 | sort | flops 36 | bytes 144 | tf_op jit(solution)/shard_map/jit(argsort)/sort | solution.py:30
  2.2 4.9 %fusion.117 = (bf16[1,2,512,512]{3,2,1,0:T(8,128)(2,1)}, bf16[2,512,512]{2,1,0:T(8,128)(2,1)S(1)}, bf16[2,512,512]{2,1,0:T(8,128)(2,1)S(1)}, bf16[2,512,512]{2,1...) fusion(f32[3,2,512,512]{3,2,1,0:T(8,128)} %param.6), kind=kLoop, calls=%fused_computation.203 | loop fusion | bytes 9437184 | tf_op jit(solution)/shard_map/slice | solution.py:70
  7.4 1.2 %fusion.73 = bf16[2,512,128]{2,0,1:T(2,128)(2,1)} fusion(bf16[2,512,128]{2,0,1:T(2,128)(2,1)S(1)} %bitcast.169, f32[2,1,1,512,128]{4,3,2,1,0:T(8,128)S(1)} %copy-done), kind=kLoop, calls=%fused_computation.111 | loop fusion | flops 393216 | bytes 1048576 | tf_op jit(solution)/shard_map/convert_element_type | solution.py:16
  8.6 1.2 %sort.47 = (s32[9]{0:T(128)}, s32[9]{0:T(128)S(1)}) sort(s32[9]{0:T(128)S(1)} %get-tuple-element.51, s32[9]{0:T(128)S(1)} %iota.24), dimensions={0}, to_apply=%region_4.6 | sort | flops 36 | bytes 144 | tf_op jit(solution)/shard_map/jit(argsort)/sort | solution.py:30
  10.0 2.4 %gather_fusion = bf16[512,2,128]{2,1,0:T(2,128)(2,1)} fusion(bf16[2,512,128]{2,0,1:T(2,128)(2,1)S(1)} %bitcast.170, s32[1024]{0:T(1024)S(1)} %get-tuple-element.61), kind=kCustom, calls=%fused_computation.clone | custom fusion | bytes 526336 | tf_op jit(solution)/shard_map/jit(_take)/gather | solution.py:44
  12.3 2.3 %gather_fusion.1 = bf16[512,2,128]{2,1,0:T(2,128)(2,1)S(1)} fusion(bf16[2,512,128]{2,0,1:T(2,128)(2,1)} %fusion.73, s32[1024]{0:T(1024)S(1)} %get-tuple-element.61), kind=kCustom, calls=%fused_computation.1.clone | custom fusion | bytes 526336 | tf_op jit(solution)/shard_map/jit(_take)/gather | solution.py:45
  14.6 3.0 %fusion.77 = (bf16[2,512,128]{2,0,1:T(2,128)(2,1)S(1)}, bf16[2,512,128]{2,0,1:T(2,128)(2,1)S(1)}) fusion(bf16[512,2,128]{2,1,0:T(2,128)(2,1)S(1)} %gather_fusion.1, pred[512]{0:T(512)(128)(4,1)S(1)} %compare_and_fusion.2, bf16[512,2,128]{2,1,0:T(2,128)(2,1)} %gather_fusion), kind=kLoop, calls=%fused_computation.134 | loop fusion | flops 262144 | bytes 1049088 | tf_op jit(solution)/shard_map/jit(_take)/select_n | solution.py:45
  18.5 5.3 %fusion.2 = (bf16[2,512,512]{2,1,0:T(8,128)(2,1)S(1)}, bf16[2,512,512]{2,1,0:T(8,128)(2,1)}, bf16[2,512,512]{2,1,0:T(8,128)(2,1)}) fusion(bf16[2,512,512]{2,1,0:T(8,128)(2,1)S(1)} %get-tuple-element.25, f32[3,2,512,512]{3,2,1,0:T(8,128)} %param.6, bf16[2,512,512]{2,1,0:T(8,128)(2,1)S(1)} %get-tuple-element.26, bf16[2,512,512]{2,1,0:T(8,128)(2,1)S(1)} %get-tuple-element.27), kind=kLoop, calls=%fused_computation.14 | loop fusion | flops 4718592 | bytes 12582912 | tf_op jit(solution)/shard_map/convert_element_type | solution.py:16
  25.1 0.8 convolution_bitcast_fusion.2
  25.9 0.8 pad_maximum_fusion
  26.7 4.2 %all-to-all-start = ((f32[2,4,128,128]{3,2,0,1:T(8,128)}), f32[2,4,128,128]{3,2,0,1:T(8,128)S(1)}, u32[]{:S(2)}, u32[]{:S(2)}) async-start(f32[2,4,128,128]{3,2,0,1:T(8,128)} %pad_maximum_fusion), calls=%async_computation | async-start | bytes 1048576 | tf_op jit(solution)/shard_map/all_to_all | solution.py:73
  31.0 1.3 %sort.46 = (s32[9]{0:T(128)}, s32[9]{0:T(128)S(1)}) sort(s32[9]{0:T(128)S(1)} %get-tuple-element.53, s32[9]{0:T(128)S(1)} %iota.23), dimensions={0}, to_apply=%region_2.0 | sort | flops 36 | bytes 144 | tf_op jit(solution)/shard_map/jit(argsort)/sort | solution.py:30
  32.3 7.5 %all-to-all-done = f32[2,4,128,128]{3,2,0,1:T(8,128)S(1)} async-done(((f32[2,4,128,128]{3,2,0,1:T(8,128)}), f32[2,4,128,128]{3,2,0,1:T(8,128)S(1)}, u32[]{:S(2)}, u32[]{:S(2)}) %all-to-all-start) | async-done | bytes 524320 | tf_op jit(solution)/shard_map/all_to_all | solution.py:73
  40.8 2.1 %gather_fusion.2 = bf16[512,2,128]{2,1,0:T(2,128)(2,1)S(1)} fusion(bf16[2,512,128]{2,0,1:T(2,128)(2,1)S(1)} %bitcast_convert_fusion.3, s32[1024]{0:T(1024)S(1)} %pad_clamp_fusion.1), kind=kCustom, calls=%fused_computation.2.clone | custom fusion | bytes 526336 | tf_op jit(solution)/shard_map/jit(_take)/gather | solution.py:44
  42.9 2.1 %gather_fusion.3 = bf16[512,2,128]{2,1,0:T(2,128)(2,1)S(1)} fusion(bf16[2,512,128]{2,0,1:T(2,128)(2,1)S(1)} %fusion.72, s32[1024]{0:T(1024)S(1)} %pad_clamp_fusion.1), kind=kCustom, calls=%fused_computation.3.clone | custom fusion | bytes 526336 | tf_op jit(solution)/shard_map/jit(_take)/gather | solution.py:45
  45.0 1.8 %fusion.79 = (bf16[2,512,128]{2,0,1:T(2,128)(2,1)S(1)}, bf16[2,512,128]{2,0,1:T(2,128)(2,1)S(1)}) fusion(bf16[512,2,128]{2,1,0:T(2,128)(2,1)S(1)} %gather_fusion.3, pred[512]{0:T(512)(128)(4,1)S(1)} %compare_and_fusion.1, bf16[512,2,128]{2,1,0:T(2,128)(2,1)S(1)} %gather_fusion.2), kind=kLoop, calls=%fused_computation.136 | loop fusion | flops 262144 | bytes 1049088 | tf_op jit(solution)/shard_map/jit(_take)/select_n | solution.py:45
  49.0 0.7 convolution_bitcast_fusion.1
  54.9 6.5 %all-to-all-start.1 = ((f32[8,2,1,64,128]{4,3,1,2,0:T(8,128)}), f32[8,2,1,64,128]{4,3,1,2,0:T(8,128)S(1)}, u32[]{:S(2)}, u32[]{:S(2)}) async-start(f32[8,2,1,64,128]{4,3,1,2,0:T(8,128)} %fusion.104), calls=%async_computation.1 | async-start | bytes 1048576 | tf_op jit(solution)/shard_map/all_to_all | solution.py:9
  61.4 14.2 %all-to-all-done.1 = f32[8,2,1,64,128]{4,3,1,2,0:T(8,128)S(1)} async-done(((f32[8,2,1,64,128]{4,3,1,2,0:T(8,128)}), f32[8,2,1,64,128]{4,3,1,2,0:T(8,128)S(1)}, u32[]{:S(2)}, u32[]{:S(2)}) %all-to-all-start.1) | async-done | bytes 524320 | tf_op jit(solution)/shard_map/all_to_all | solution.py:9
  76.3 2.1 %gather_fusion.5 = bf16[512,2,128]{2,1,0:T(2,128)(2,1)S(1)} fusion(bf16[2,512,128]{2,0,1:T(2,128)(2,1)S(1)} %copy.137, s32[1024]{0:T(1024)S(1)} %get-tuple-element.60), kind=kCustom, calls=%fused_computation.5.clone | custom fusion | bytes 526336 | tf_op jit(solution)/shard_map/jit(_take)/gather | solution.py:45
  78.4 2.1 %gather_fusion.4 = bf16[512,2,128]{2,1,0:T(2,128)(2,1)S(1)} fusion(bf16[2,512,128]{2,0,1:T(2,128)(2,1)S(1)} %copy.136, s32[1024]{0:T(1024)S(1)} %get-tuple-element.60), kind=kCustom, calls=%fused_computation.4.clone | custom fusion | bytes 526336 | tf_op jit(solution)/shard_map/jit(_take)/gather | solution.py:44
  80.6 1.8 %fusion.81 = (bf16[2,512,128]{2,0,1:T(2,128)(2,1)S(1)}, bf16[2,512,128]{2,0,1:T(2,128)(2,1)S(1)}) fusion(bf16[512,2,128]{2,1,0:T(2,128)(2,1)S(1)} %gather_fusion.5, pred[512]{0:T(512)(128)(4,1)S(1)} %compare_and_fusion, bf16[512,2,128]{2,1,0:T(2,128)(2,1)S(1)} %gather_fusion.4), kind=kLoop, calls=%fused_computation.138 | loop fusion | flops 262144 | bytes 1049088 | tf_op jit(solution)/shard_map/jit(_take)/select_n | solution.py:45
  85.7 1.0 %copy.140 = f32[2,1,1,512,128]{4,3,2,1,0:T(8,128)} copy(f32[2,1,1,512,128]{3,4,0,2,1:T(8,128)S(1)} %maximum_bitcast_fusion) | data formatting | bytes 1048576 | tf_op jit(solution)/shard_map/reshape | solution.py:80
  (69 shorter events, 15.0 us)
Async XLA Ops:
  2.2 4.9 %copy-start = (f32[2,1,1,512,128]{4,3,2,1,0:T(8,128)S(1)}, f32[2,1,1,512,128]{4,3,2,1,0:T(8,128)}, u32[]{:S(2)}) copy-start(f32[2,1,1,512,128]{4,3,2,1,0:T(8,128)} %param.5) | copy-start | bytes 1572868
  23.8 1.2 %copy-start.5 = (bf16[1,2,512,512]{3,2,1,0:T(8,128)(2,1)S(1)}, bf16[1,2,512,512]{3,2,1,0:T(8,128)(2,1)}, u32[]{:S(2)}) copy-start(bf16[1,2,512,512]{3,2,1,0:T(8,128)(2,1)} %get-tuple-element.28) | copy-start | bytes 3145732
  26.7 13.1 %all-to-all-start = ((f32[2,4,128,128]{3,2,0,1:T(8,128)}), f32[2,4,128,128]{3,2,0,1:T(8,128)S(1)}, u32[]{:S(2)}, u32[]{:S(2)}) async-start(f32[2,4,128,128]{3,2,0,1:T(8,128)} %pad_maximum_fusion), calls=%async_computation | async-start | bytes 1048576 | tf_op jit(solution)/shard_map/all_to_all | solution.py:73
  46.8 1.2 %copy-start.4 = (bf16[2,512,512]{2,1,0:T(8,128)(2,1)S(1)}, bf16[2,512,512]{2,1,0:T(8,128)(2,1)}, u32[]{:S(2)}) copy-start(bf16[2,512,512]{2,1,0:T(8,128)(2,1)} %get-tuple-element.31) | copy-start | bytes 3145732
  47.7 1.3 %copy-start.3 = (bf16[1,2,512,512]{3,2,1,0:T(8,128)(2,1)S(1)}, bf16[1,2,512,512]{3,2,1,0:T(8,128)(2,1)}, u32[]{:S(2)}) copy-start(bf16[1,2,512,512]{3,2,1,0:T(8,128)(2,1)} %get-tuple-element.29) | copy-start | bytes 3145732
  54.9 20.7 %all-to-all-start.1 = ((f32[8,2,1,64,128]{4,3,1,2,0:T(8,128)}), f32[8,2,1,64,128]{4,3,1,2,0:T(8,128)S(1)}, u32[]{:S(2)}, u32[]{:S(2)}) async-start(f32[8,2,1,64,128]{4,3,1,2,0:T(8,128)} %fusion.104), calls=%async_computation.1 | async-start | bytes 1048576 | tf_op jit(solution)/shard_map/all_to_all | solution.py:9
  82.4 1.2 %copy-start.2 = (bf16[2,512,512]{2,1,0:T(8,128)(2,1)S(1)}, bf16[2,512,512]{2,1,0:T(8,128)(2,1)}, u32[]{:S(2)}) copy-start(bf16[2,512,512]{2,1,0:T(8,128)(2,1)} %get-tuple-element.32) | copy-start | bytes 3145732
  83.6 1.2 %copy-start.1 = (bf16[1,2,512,512]{3,2,1,0:T(8,128)(2,1)S(1)}, bf16[1,2,512,512]{3,2,1,0:T(8,128)(2,1)}, u32[]{:S(2)}) copy-start(bf16[1,2,512,512]{3,2,1,0:T(8,128)(2,1)} %get-tuple-element.24) | copy-start | bytes 3145732
